TPU v7x, 256 devices: a whole 4x4x8 slice. The times are simulated.
256 devices in a mesh: chan: 32 (over z_lo, x, core), inp: 8 (over z_hi, y).
Axes of the slice: x: 4, y: 4, z: 8 (z_hi: 2, z_lo: 4; z = z_hi * 4 + z_lo), core: 2. Of those that a mesh axis runs over, the one named last changes fastest.
Arguments:
- voltages: bfloat16 [512, 2, 131072], P('inp', None, 'chan'), may hold values from -64 to 64
Outputs:
- delays: float32 [512, 512, 2, 512], P('inp', 'chan')
All inputs are finite; a program needn't handle non-finite values.
Results may differ from a plain program's by a relative error of at most 0.0053.
Values may be sent and summed in bfloat16 or wider, within the bound.
No kernel may reach another device: no remote copies, remote signals or barrier semaphores. Data moves between devices by JAX's collectives and lax.ppermute only.
A program may use at most 128 MiB of HBM per device.

v0:
```python
import math
import jax
import jax.numpy as jnp
from jax import lax
from jax.sharding import PartitionSpec as P

NCH = 512


def taper_weights(count):
    position = jnp.arange(count, dtype=jnp.float32)
    return 0.5 - 0.5 * jnp.cos(2.0 * math.pi * (position + 0.5) / count)


def channel_table(count):
    indices = jnp.arange(count, dtype=jnp.int32)
    product = indices[:, None] * indices[None, :] % count
    angle = 2.0 * math.pi / count * product.astype(jnp.float32)
    window = taper_weights(count)[:, None] / math.sqrt(count)
    cosine = window * jnp.cos(angle)
    sine = window * jnp.sin(angle)
    upper = jnp.concatenate([cosine, -sine], axis=1)
    lower = jnp.concatenate([sine, cosine], axis=1)
    return jnp.concatenate([upper, lower], axis=0).astype(jnp.bfloat16)


def dft_tables(row_count, col_count, modulus):
    row_idx = jnp.arange(row_count, dtype=jnp.int32)
    col_idx = jnp.arange(col_count, dtype=jnp.int32)
    angle = (
        2.0
        * math.pi
        / modulus
        * (row_idx[:, None] * col_idx[None, :] % modulus).astype(jnp.float32)
    )
    return (jnp.cos(angle), jnp.sin(angle))


def complex_section(real_in, imag_in, cosine, sine, form):
    highest = lax.Precision.HIGHEST
    real_out = jnp.einsum(form, cosine, real_in, precision=highest) + jnp.einsum(
        form, sine, imag_in, precision=highest
    )
    imag_out = jnp.einsum(form, cosine, imag_in, precision=highest) - jnp.einsum(
        form, sine, real_in, precision=highest
    )
    return (real_out, imag_out)


def rotate(real_in, imag_in, cosine, sine):
    return (real_in * cosine + imag_in * sine, imag_in * cosine - real_in * sine)


def shards(voltages):
    input_rows = voltages.shape[0]
    local_time = voltages.shape[2]
    chan_count = lax.axis_size("chan")
    spec_local = local_time // NCH
    chan_local = NCH // chan_count
    table = channel_table(NCH)
    table = (
        table.reshape(2 * NCH, 2, chan_local, chan_count)
        .transpose(0, 1, 3, 2)
        .reshape(2 * NCH, 2 * NCH)
    )
    samples = (
        voltages.reshape(input_rows, 2, spec_local, NCH)
        .transpose(0, 2, 1, 3)
        .reshape(input_rows * spec_local, 2 * NCH)
    )
    spectra = jnp.dot(samples, table, preferred_element_type=jnp.float32).astype(jnp.bfloat16)
    spectra = spectra.reshape(input_rows, spec_local, 2, NCH)
    turned = lax.all_to_all(spectra, "chan", split_axis=3, concat_axis=1, tiled=True)
    spec_total = turned.shape[1]
    mine = turned.transpose(3, 0, 2, 1).reshape(chan_local, input_rows, 2 * spec_total)
    own_power = jnp.sum(jnp.square(mine.astype(jnp.float32)), axis=2) / spec_total + 1e-06
    own_scale = lax.rsqrt(own_power)
    piece = lax.all_gather(mine, "inp", axis=1, tiled=True)
    half = piece.shape[2] // 2
    rotated = jnp.concatenate([-piece[:, :, half:], piece[:, :, :half]], axis=2)
    numbers = (((2,), (2,)), ((0,), (0,)))
    real_part = lax.dot_general(mine, piece, numbers, preferred_element_type=jnp.float32)
    imag_part = lax.dot_general(mine, rotated, numbers, preferred_element_type=jnp.float32)
    power = jnp.sum(jnp.square(piece.astype(jnp.float32)), axis=2) / spec_total + 1e-06
    scaling = own_scale[:, :, None] * lax.rsqrt(power)[:, None, :] / spec_total
    rho = jnp.stack([real_part * scaling, imag_part * scaling], axis=1).astype(jnp.bfloat16)
    col_local = rho.shape[3] // chan_count
    baseline_count = input_rows * col_local
    chan_index = lax.axis_index("chan")
    position = (chan_count * jnp.arange(chan_local, dtype=jnp.int32) + chan_index).astype(
        jnp.float32
    )
    taper_local = 0.5 - 0.5 * jnp.cos(2.0 * math.pi * (position + 0.5) / NCH)
    weighted = rho.astype(jnp.float32) * taper_local[:, None, None, None]
    cos_first, sin_first = dft_tables(chan_local, chan_local, chan_local)
    section_real, section_imag = complex_section(
        weighted[:, 0], weighted[:, 1], cos_first, sin_first, "ka,aij->kij"
    )
    twist = (
        2.0
        * math.pi
        / NCH
        * (chan_index * jnp.arange(chan_local, dtype=jnp.int32) % NCH).astype(jnp.float32)
    )
    section_real, section_imag = rotate(
        section_real, section_imag, jnp.cos(twist)[:, None, None], jnp.sin(twist)[:, None, None]
    )
    paired = jnp.stack([section_real, section_imag], axis=1)
    arranged = paired.reshape(chan_local, 2, input_rows, chan_count, col_local).transpose(
        3, 0, 1, 2, 4
    )
    arranged = arranged.reshape(chan_count, chan_local, 2, baseline_count)
    regrouped = lax.all_to_all(arranged, "chan", split_axis=0, concat_axis=0, tiled=True)
    cos_second, sin_second = dft_tables(chan_count, chan_count, chan_count)
    out_real, out_imag = complex_section(
        regrouped[:, :, 0], regrouped[:, :, 1], cos_second, sin_second, "mb,bkn->mkn"
    )
    factor = math.sqrt(spec_total / NCH)
    combined = (
        jnp.stack(
            [out_real.reshape(NCH, baseline_count), out_imag.reshape(NCH, baseline_count)], axis=0
        )
        * factor
    )
    result = combined.transpose(2, 0, 1).reshape(input_rows, col_local, 2, NCH)
    rows_global = lax.axis_index("inp") * input_rows + jnp.arange(input_rows, dtype=jnp.int32)
    cols_global = lax.axis_index("chan") * col_local + jnp.arange(col_local, dtype=jnp.int32)
    same = rows_global[:, None] == cols_global[None, :]
    return jnp.where(same[:, :, None, None], jnp.zeros_like(result), result)


def solution(mesh):
    in_specs = (P("inp", None, "chan"),)
    out_specs = P("inp", "chan", None, None)
    return jax.shard_map(shards, mesh=mesh, in_specs=in_specs, out_specs=out_specs, check_vma=False)
```

profile of v0, /device:TPU:1, one launch (start us, length us, event | category | flops | bytes accessed | tf_op | source)
XLA Modules:
  0.0 456.4 jit_solution(16119081496924792960)
XLA Ops:
  6.6 1.8 reshape.197
  8.4 4.7 %negate_convert_fusion = (bf16[512,1,16,32]{0,2,3,1:T(8,128)(2,1)S(1)}, bf16[512,1,16,32]{0,2,3,1:T(8,128)(2,1)S(1)}, bf16[512,1,16,32]{0,2,3,1:T(8,128)(2,1)S(1)}) fusion(s32[16,32]{0,1:T(8,128)S(1)} %multiply_add_fusion.1, f32[512]{0:T(512)S(1)} %subtract_multiply_fusion), kind=kLoop, calls=%fused_computation.48 | loop fusion | flops 5242880 | bytes 1576960 | tf_op jit(solution)/shard_map/convert.9
  13.1 0.3 maximum_maximum_fusion
  13.4 1.3 fusion.28
  14.7 0.5 copy.57
  15.2 0.8 reshape.199
  16.0 2.9 copy.58
  18.9 1.5 reshape.207
  20.4 36.5 %all_to_all.23 = bf16[32,2,8192]{2,1,0:T(2,128)(2,1)S(1)} all-to-all(bf16[32,2,8192]{2,1,0:T(2,128)(2,1)S(1)} %reshape.207), channel_id=1, replica_groups=mesh['chan'=32,'inp'=8] {'chan'}, dimensions={0} | all-to-all | bytes 2097152 | tf_op jit(solution)/shard_map/all_to_all | solution.py:73
  56.8 2.3 reshape.208
  59.1 2.1 copy.60
  61.3 2.7 copy.61
  64.0 1.5 reshape.200
  65.5 0.0 all-gather.2.cloned.1.call-update
  65.6 0.1 fusion.74
  65.6 0.7 multiply_reduce_fusion.1
  66.4 170.8 %all-gather.2.cloned.1.call-done = bf16[16,512,512]{2,1,0:T(8,128)(2,1)} async-done(((bf16[16,64,512]{2,1,0:T(8,128)(2,1)}), bf16[16,512,512]{2,1,0:T(8,128)(2,1)}) %all-gather.2.cloned.1.call-update) | async-done | bytes 8388624 | tf_op jit(solution)/shard_map/all_gather | solution.py:78
  237.1 5.3 %multiply_reduce_fusion = f32[16,512]{1,0:T(8,128)S(1)} fusion(bf16[16,512,512]{2,1,0:T(8,128)(2,1)} %all-gather.2.cloned.1.call-done), kind=kLoop, calls=%fused_computation | loop fusion | flops 12574720 | bytes 8421376 | tf_op jit(solution)/shard_map/reduce_sum | solution.py:84
  242.4 0.5 copy-done
  242.9 0.6 slice_negate_fusion
  243.5 0.6 copy-done.1
  244.1 3.0 fusion.29
  247.2 2.6 fusion.27
  249.8 0.7 convert_multiply_fusion
  250.5 0.7 slice_bitcast_fusion.1
  251.2 2.9 fusion.11
  254.1 2.9 fusion.9
  257.0 2.9 fusion.17
  259.9 17.3 %multiply_add_fusion = (f32[16,64,512]{2,0,1:T(8,128)}, f32[16,64,512]{2,0,1:T(8,128)S(1)}) fusion(f32[16,64,512]{2,0,1:T(8,128)S(1)} %fusion.17, f32[16]{0:T(128)S(1)} %get-tuple-element.16, f32[16]{0:T(128)S(1)} %get-tuple-element.17, f32[16,64,512]{2,0,1:T(8,128)S(1)} %fusion.9, f32[16,64,512]{2,1,0:T(8,128)S(1)} %get-tuple-element.11), kind=kOutput, calls=%fused_computation.17 | convolution fusion | flops 104336896 | bytes 10485888 | tf_op jit(solution)/shard_map/ka,aij->kij/dot_general | solution.py:44
  277.3 3.8 copy.66
  281.1 2.8 copy.67
  283.8 7.6 %maximum_bitcast_fusion = f32[32,16,2,64,16]{3,4,0,1,2:T(8,128)} fusion(f32[16,1,64,32,16]{2,4,3,0,1:T(8,128)} %bitcast.78, f32[16,1,64,32,16]{2,4,3,0,1:T(8,128)} %bitcast.77), kind=kLoop, calls=%fused_computation.5 | loop fusion | flops 1048576 | bytes 8388608 | tf_op jit(solution)/shard_map/transpose | solution.py:109
  291.5 13.4 %copy.68 = f32[32,16,2,64,16]{0,4,3,2,1:T(8,128)} copy(f32[32,16,2,64,16]{3,4,0,1,2:T(8,128)} %maximum_bitcast_fusion) | data formatting | bytes 8388608 | tf_op jit(solution)/shard_map/transpose | solution.py:109
  304.8 11.7 %copy.69 = f32[32,16,2,1024]{3,1,2,0:T(8,128)} copy(f32[32,16,2,1024]{0,3,2,1:T(8,128)} %bitcast.74) | data formatting | bytes 8388608 | tf_op jit(solution)/shard_map/reshape | solution.py:112
  316.6 5.9 %all-to-all-start.1 = ((f32[32,16,2,1024]{3,1,2,0:T(8,128)}), f32[32,16,2,1024]{3,1,2,0:T(8,128)}, u32[]{:S(2)}, u32[]{:S(2)}) async-start(f32[32,16,2,1024]{3,1,2,0:T(8,128)} %copy.69), calls=%async_computation.1 | async-start | bytes 8388608 | tf_op jit(solution)/shard_map/all_to_all | solution.py:113
  322.5 0.1 broadcast_compare_fusion
  322.5 93.0 %all-to-all-done.1 = f32[32,16,2,1024]{3,1,2,0:T(8,128)} async-done(((f32[32,16,2,1024]{3,1,2,0:T(8,128)}), f32[32,16,2,1024]{3,1,2,0:T(8,128)}, u32[]{:S(2)}, u32[]{:S(2)}) %all-to-all-start.1) | async-done | bytes 4194336 | tf_op jit(solution)/shard_map/all_to_all | solution.py:113
  415.6 2.5 fusion.109
  418.1 3.0 fusion.6
  421.2 3.0 fusion.5
  424.2 3.0 fusion.23
  427.2 1.2 copy.72
  428.4 3.2 fusion.24
  431.7 1.2 copy.73
  432.9 2.5 fusion.4
  435.4 5.4 %copy.74 = f32[1024,2,512]{2,0,1:T(8,128)} copy(f32[1024,2,512]{0,2,1:T(8,128)} %fusion.4) | data formatting | bytes 8388608 | tf_op jit(solution)/shard_map/transpose | solution.py:125
  440.8 2.5 broadcast_select_fusion
  443.3 5.8 %copy.75 = f32[64,16,2,512]{3,2,1,0:T(2,128)} copy(f32[64,16,2,512]{3,1,0,2:T(8,128)S(1)} %broadcast_select_fusion) | data formatting | bytes 8388608 | tf_op jit(solution)/shard_map/jit(_where)/select_n | solution.py:129
  (10 shorter events, 0.1 us)
Async XLA Ops:
  6.5 230.6 %all-gather.2.cloned.1.call-start = ((), (), s32[]{:S(2)}) async-start(), calls=%async_computation.2 | async-start | bytes 9437184 | tf_op jit(solution)/shard_map/all_gather | solution.py:78
  237.1 5.8 %copy-start = (bf16[16,512,512]{2,1,0:T(8,128)(2,1)S(1)}, bf16[16,512,512]{2,1,0:T(8,128)(2,1)}, u32[]{:S(2)}) copy-start(bf16[16,512,512]{2,1,0:T(8,128)(2,1)} %all-gather.2.cloned.1.call-done) | copy-start | bytes 25165828
  242.9 1.2 copy-start.1
  316.6 99.0 %all-to-all-start.1 = ((f32[32,16,2,1024]{3,1,2,0:T(8,128)}), f32[32,16,2,1024]{3,1,2,0:T(8,128)}, u32[]{:S(2)}, u32[]{:S(2)}) async-start(f32[32,16,2,1024]{3,1,2,0:T(8,128)} %copy.69), calls=%async_computation.1 | async-start | bytes 8388608 | tf_op jit(solution)/shard_map/all_to_all | solution.py:113
Sparse Core Ops, SparseCore 0:
  65.6 171.4 all-gather.1
where the time goes:
time: 465 us; the launch traced here: 456 us
  waiting for transfers between devices  264 us (57%)
  local copies, waits for them, and re-layouts  65.8 us (14%)
  matrix products  45.3 us (10%)
  blocking collectives  36.5 us (8%)
  other arithmetic  25.2 us (5%)
  between operations  14 us (3%)
  starting transfers between devices  5.88 us (1%)
    all_gather x1, waiting for transfers between devices, shards(): piece = lax.all_gather(mine, 'inp', axis=1, tiled=True)  171 us
    all_to_all x1, waiting for transfers between devices, shards(): lax.all_to_all(arranged, 'chan', split_axis=0, concat_axis=0, tiled=True)  93 us
    all_to_all x1, blocking collectives, shards(): lax.all_to_all(spectra, 'chan', split_axis=3, concat_axis=1, tiled=True)  36.5 us
    dot_general x2, matrix products, complex_section(): jnp.einsum(form, sine, real_in, precision=highest)  20.4 us
    transpose x1, local copies, waits for them, and re-layouts, shards(): paired.reshape(chan_local, 2, input_rows, chan_count, col_local)  13.4 us
    reshape x1, local copies, waits for them, and re-layouts, shards(): arranged = arranged.reshape(chan_count, chan_local, 2, baseline_count)  11.7 us
  transfers between devices with their start and end apart: 2, of which 2 were waited for; matrix products, arithmetic and copies ran while one was open for 0% of the time, Pallas kernels for 0%

commit v1 on v0

--- a/solution.py
+++ b/solution.py
@@ -75,7 +75,8 @@
     mine = turned.transpose(3, 0, 2, 1).reshape(chan_local, input_rows, 2 * spec_total)
     own_power = jnp.sum(jnp.square(mine.astype(jnp.float32)), axis=2) / spec_total + 1e-06
     own_scale = lax.rsqrt(own_power)
-    piece = lax.all_gather(mine, "inp", axis=1, tiled=True)
+    repeated = jnp.stack([mine] * lax.axis_size("inp"))
+    piece = jnp.concatenate(lax.all_to_all(repeated, "inp", 0, 0), axis=1)
     half = piece.shape[2] // 2
     rotated = jnp.concatenate([-piece[:, :, half:], piece[:, :, :half]], axis=2)
     numbers = (((2,), (2,)), ((0,), (0,)))

time: 465 us -> 480 us (1.032)
  waiting for transfers between devices: 264 us -> 279 us
  between operations: 14 us -> 0.45 us
  local copies, waits for them, and re-layouts: 65.8 us -> 79.2 us
  matrix products: 45.3 us -> 33.1 us
  starting transfers between devices: 5.88 us -> 13.8 us
    all_to_all x0 -> x1, waiting for transfers between devices: none -> 186 us  [shards(): piece = jnp.concatenate(lax.all_to_all(repeated, 'inp', 0, 0), axis=1)]
    all_gather x1 -> x0, waiting for transfers between devices: 171 us -> none  [shards(): piece = lax.all_gather(mine, 'inp', axis=1, tiled=True)]
    dot_general x2, matrix products: 20.4 us -> 8.17 us  [complex_section(): jnp.einsum(form, sine, real_in, precision=highest)]
    all_to_all x0 -> x1, starting transfers between devices: none -> 8.35 us  [shards(): piece = jnp.concatenate(lax.all_to_all(repeated, 'inp', 0, 0), axis=1)]
    reshape x0 -> x1, local copies, waits for them, and re-layouts: none -> 7.71 us  [shards(): piece = jnp.concatenate(lax.all_to_all(repeated, 'inp', 0, 0), axis=1)]
where the time goes in v1:
time: 480 us; the launch traced here: 470 us
  waiting for transfers between devices  279 us (58%)
  local copies, waits for them, and re-layouts  79.2 us (16%)
  blocking collectives  36.5 us (8%)
  matrix products  33.1 us (7%)
  other arithmetic  28.3 us (6%)
  starting transfers between devices  13.8 us (3%)
    all_to_all x1, waiting for transfers between devices, shards(): piece = jnp.concatenate(lax.all_to_all(repeated, 'inp', 0, 0), axis=1)  186 us
    all_to_all x1, waiting for transfers between devices, shards(): lax.all_to_all(arranged, 'chan', split_axis=0, concat_axis=0, tiled=True)  93.1 us
    all_to_all x1, blocking collectives, shards(): lax.all_to_all(spectra, 'chan', split_axis=3, concat_axis=1, tiled=True)  36.5 us
    transpose x1, local copies, waits for them, and re-layouts, shards(): paired.reshape(chan_local, 2, input_rows, chan_count, col_local)  13.4 us
    reshape x1, local copies, waits for them, and re-layouts, shards(): arranged = arranged.reshape(chan_count, chan_local, 2, baseline_count)  11.7 us
  transfers between devices with their start and end apart: 2, of which 2 were waited for; matrix products, arithmetic and copies ran while one was open for 0% of the time, Pallas kernels for 0%

profile of v1, /device:TPU:1, one launch (start us, length us, event | category | flops | bytes accessed | tf_op | source)
XLA Modules:
  0.0 470.3 jit_solution(12760320987310178632)
XLA Ops:
  0.1 1.8 reshape.214
  1.9 4.7 negate_convert_fusion
  6.5 0.3 maximum_maximum_fusion
  6.9 1.3 fusion.28
  8.2 0.5 copy.78
  8.7 0.8 reshape.216
  9.5 2.9 copy.79
  12.4 1.5 reshape.226
  13.9 36.5 %all_to_all.28 = bf16[32,2,8192]{2,1,0:T(2,128)(2,1)S(1)} all-to-all(bf16[32,2,8192]{2,1,0:T(2,128)(2,1)S(1)} %reshape.226), channel_id=1, replica_groups=mesh['chan'=32,'inp'=8] {'chan'}, dimensions={0} | all-to-all | bytes 2097152 | tf_op jit(solution)/shard_map/all_to_all | solution.py:73
  50.3 2.3 reshape.227
  52.6 2.1 copy.81
  54.7 3.0 copy.82
  57.8 1.7 reshape.217
  59.5 4.3 stack.27
  63.8 8.3 %all-to-all-start.1 = ((bf16[8,16,64,512]{3,2,1,0:T(8,128)(2,1)}), bf16[8,16,64,512]{3,2,1,0:T(8,128)(2,1)}, u32[]{:S(2)}, u32[]{:S(2)}) async-start(bf16[8,16,64,512]{3,2,1,0:T(8,128)(2,1)} %stack.27), calls=%async_computation.1 | async-start | bytes 16777216 | tf_op jit(solution)/shard_map/all_to_all | solution.py:79
  72.3 0.7 multiply_reduce_fusion.1
  73.0 185.8 %all-to-all-done.1 = bf16[8,16,64,512]{3,2,1,0:T(8,128)(2,1)} async-done(((bf16[8,16,64,512]{3,2,1,0:T(8,128)(2,1)}), bf16[8,16,64,512]{3,2,1,0:T(8,128)(2,1)}, u32[]{:S(2)}, u32[]{:S(2)}) %all-to-all-start.1) | async-done | bytes 8388640 | tf_op jit(solution)/shard_map/all_to_all | solution.py:79
  258.9 5.1 %multiply_reduce_fusion = f32[16,8,64]{2,0,1:T(8,128)S(1)} fusion(bf16[8,16,64,512]{3,2,1,0:T(8,128)(2,1)} %all-to-all-done.1), kind=kLoop, calls=%fused_computation | loop fusion | flops 12574720 | bytes 8421376 | tf_op jit(solution)/shard_map/reduce_sum | solution.py:85
  264.0 0.1 rsqrt.19
  264.1 7.7 %copy.83 = bf16[16,8,64,512]{3,2,1,0:T(8,128)(2,1)} copy(bf16[16,8,64,512]{3,2,0,1:T(8,128)(2,1)} %bitcast.12) | data formatting | bytes 16777216 | tf_op jit(solution)/shard_map/reshape | solution.py:79
  271.8 3.9 slice_negate_fusion
  275.7 1.9 copy-done
  277.7 2.6 fusion.27
  280.3 3.0 fusion.29
  283.3 0.7 convert_multiply_fusion
  284.0 0.7 slice_bitcast_fusion.1
  284.7 2.9 fusion.9
  287.6 2.9 fusion.11
  290.5 2.9 fusion.17
  293.4 5.2 %multiply_add_fusion = (f32[16,64,512]{2,0,1:T(8,128)}, f32[16,64,512]{2,0,1:T(8,128)S(1)}) fusion(f32[16,64,512]{2,0,1:T(8,128)S(1)} %fusion.17, f32[16]{0:T(128)S(1)} %get-tuple-element.17, f32[16]{0:T(128)S(1)} %fusion.75, f32[16,64,512]{2,0,1:T(8,128)S(1)} %fusion.9, f32[16,64,512]{2,1,0:T(8,128)S(1)} %get-tuple-element.11), kind=kOutput, calls=%fused_computation.17 | convolution fusion | flops 104336896 | bytes 10485888 | tf_op jit(solution)/shard_map/ka,aij->kij/dot_general | solution.py:44
  298.6 3.8 copy.89
  302.4 2.8 copy.90
  305.2 7.6 %maximum_bitcast_fusion = f32[32,16,2,64,16]{3,4,0,1,2:T(8,128)} fusion(f32[16,1,64,32,16]{2,4,3,0,1:T(8,128)} %bitcast.83, f32[16,1,64,32,16]{2,4,3,0,1:T(8,128)} %bitcast.82), kind=kLoop, calls=%fused_computation.5 | loop fusion | flops 1048576 | bytes 8388608 | tf_op jit(solution)/shard_map/transpose | solution.py:110
  312.8 13.4 %copy.91 = f32[32,16,2,64,16]{0,4,3,2,1:T(8,128)} copy(f32[32,16,2,64,16]{3,4,0,1,2:T(8,128)} %maximum_bitcast_fusion) | data formatting | bytes 8388608 | tf_op jit(solution)/shard_map/transpose | solution.py:110
  326.2 11.7 %copy.92 = f32[32,16,2,1024]{3,1,2,0:T(8,128)} copy(f32[32,16,2,1024]{0,3,2,1:T(8,128)} %bitcast.79) | data formatting | bytes 8388608 | tf_op jit(solution)/shard_map/reshape | solution.py:113
  337.9 5.5 %all-to-all-start.2 = ((f32[32,16,2,1024]{3,1,2,0:T(8,128)}), f32[32,16,2,1024]{3,1,2,0:T(8,128)}, u32[]{:S(2)}, u32[]{:S(2)}) async-start(f32[32,16,2,1024]{3,1,2,0:T(8,128)} %copy.92), calls=%async_computation.2 | async-start | bytes 8388608 | tf_op jit(solution)/shard_map/all_to_all | solution.py:114
  343.4 93.1 %all-to-all-done.2 = f32[32,16,2,1024]{3,1,2,0:T(8,128)} async-done(((f32[32,16,2,1024]{3,1,2,0:T(8,128)}), f32[32,16,2,1024]{3,1,2,0:T(8,128)}, u32[]{:S(2)}, u32[]{:S(2)}) %all-to-all-start.2) | async-done | bytes 4194336 | tf_op jit(solution)/shard_map/all_to_all | solution.py:114
  436.5 2.5 fusion.109
  439.0 3.0 fusion.5
  442.1 3.0 fusion.6
  445.1 3.0 fusion.23
  448.1 3.2 fusion.24
  451.4 1.2 copy.96
  452.6 1.2 copy.95
  453.8 2.5 fusion.4
  456.3 5.4 %copy.97 = f32[1024,2,512]{2,0,1:T(8,128)} copy(f32[1024,2,512]{0,2,1:T(8,128)} %fusion.4) | data formatting | bytes 8388608 | tf_op jit(solution)/shard_map/transpose | solution.py:126
  461.7 2.5 broadcast_select_fusion
  464.3 5.8 %copy.98 = f32[64,16,2,512]{3,2,1,0:T(2,128)} copy(f32[64,16,2,512]{3,1,0,2:T(8,128)S(1)} %broadcast_select_fusion) | data formatting | bytes 8388608 | tf_op jit(solution)/shard_map/jit(_where)/select_n | solution.py:130
  (11 shorter events, 0.3 us)
Async XLA Ops:
  63.8 195.1 %all-to-all-start.1 = ((bf16[8,16,64,512]{3,2,1,0:T(8,128)(2,1)}), bf16[8,16,64,512]{3,2,1,0:T(8,128)(2,1)}, u32[]{:S(2)}, u32[]{:S(2)}) async-start(bf16[8,16,64,512]{3,2,1,0:T(8,128)(2,1)} %stack.27), calls=%async_computation.1 | async-start | bytes 16777216 | tf_op jit(solution)/shard_map/all_to_all | solution.py:79
  271.8 5.8 %copy-start = (bf16[16,8,64,512]{3,2,1,0:T(8,128)(2,1)S(1)}, bf16[16,8,64,512]{3,2,1,0:T(8,128)(2,1)}, u32[]{:S(2)}) copy-start(bf16[16,8,64,512]{3,2,1,0:T(8,128)(2,1)} %copy.83) | copy-start | bytes 25165828
  337.9 98.6 %all-to-all-start.2 = ((f32[32,16,2,1024]{3,1,2,0:T(8,128)}), f32[32,16,2,1024]{3,1,2,0:T(8,128)}, u32[]{:S(2)}, u32[]{:S(2)}) async-start(f32[32,16,2,1024]{3,1,2,0:T(8,128)} %copy.92), calls=%async_computation.2 | async-start | bytes 8388608 | tf_op jit(solution)/shard_map/all_to_all | solution.py:114
